TPU v7x, 32 devices: a whole 2x2x4 slice. The times are simulated.
32 devices in a mesh: groups: 2 (over y), tok: 4 (over z), head: 2 (over x), rep: 2 (over core).
Axes of the slice: x: 2, y: 2, z: 4, core: 2. Of those that a mesh axis runs over, the one named last changes fastest.
Arguments:
- keys: bfloat16 [1024, 1024], P(('groups', 'tok'), 'head'), parts along dimension 0, may hold values from -6 to 6
- values: bfloat16 [1024, 1024], P(('groups', 'tok'), 'head'), parts along dimension 0, may hold values from -6 to 6
- rates: float32 [1024, 2], P(('groups', 'tok'), 'head'), parts along dimension 0, may hold values from 0.0003 to 0.006
- queries: bfloat16 [1024, 1024], P(('groups', 'tok'), 'head'), parts along dimension 0, may hold values from -6 to 6
- stream: bfloat16 [1024, 1024], P(('groups', 'tok'), 'head'), parts along dimension 0, may hold values from -16 to 16
- gain: float32 [1024], P('head'), may hold values from 0.1 to 1.9
- counts: int32 [8], P(('groups', 'tok')), parts along dimension 0, may hold values from 1 to 128, 307 in all
- fw_one: float32 [2, 512, 1024], P('head', None, 'rep'), may hold values from -0.25 to 0.25
- fw_three: float32 [2, 512, 1024], P('head', None, 'rep'), may hold values from -0.25 to 0.25
- fw_two: float32 [2, 1024, 512], P('head', 'rep'), may hold values from -1 to 1
- mlp_up: bfloat16 [1024, 4096], P('tok', ('head', 'rep')), may hold values from -0.1875 to 0.1875
- mlp_down: bfloat16 [4096, 1024], P(('head', 'rep'), 'tok'), may hold values from -0.09375 to 0.09375
Outputs:
- result: bfloat16 [1024, 1024], P(('groups', 'tok'), ('head', 'rep')), parts along dimension 0
There are 2 independent parts, one for each index of `groups`. A program takes and returns all parts, laid end to end along the dimension named above; an argument that names none is the same for every part. Nothing has to cross between parts.
Inputs may be any that keep to these rules, and one draw needn't show every extreme that they name: counts sum to 307, and one index of tok is full.
All inputs are finite; a program needn't handle non-finite values. No bound on the sum of `counts` on one device may be relied on, other than what follows from the above.
Results may differ from a plain program's by a relative error of at most 0.04.
Values may be sent and summed in bfloat16 or wider, within the bound.
No kernel may reach another device: no remote copies, remote signals or barrier semaphores. Data moves between devices by JAX's collectives and lax.ppermute only.
A program may use at most 64 MiB of HBM per device.

v0:
```python
import jax
import jax.numpy as jnp
from jax import lax
from jax.sharding import PartitionSpec as P


def swish_parts(pre_act):
    sigmoid_val = jax.nn.sigmoid(pre_act)
    return (pre_act * sigmoid_val, sigmoid_val * (1.0 + pre_act * (1.0 - sigmoid_val)))


def column_squares(former, updated, gate_cols):
    left_old = former[:, :gate_cols]
    left_new = updated[:, :gate_cols]
    return (jnp.sum(left_old * left_old, axis=0), jnp.sum(left_new * left_new, axis=0))


def rescale(former, updated, col_former, col_updated):
    gate_cols = col_former.shape[0]
    right_old = former[:, gate_cols:]
    right_new = updated[:, gate_cols:]
    row_sums = lax.psum(
        (jnp.sum(right_old * right_old, axis=1), jnp.sum(right_new * right_new, axis=1)), "rep"
    )
    left_part = updated[:, :gate_cols] * jnp.sqrt(col_former) * lax.rsqrt(col_updated + 1e-06)
    row_factor = jnp.sqrt(row_sums[0]) * lax.rsqrt(row_sums[1] + 1e-06)
    right_part = right_new * row_factor[:, None]
    return jnp.concatenate([left_part, right_part], axis=1).astype(jnp.bfloat16)


def on_device(
    keys, values, rates, queries, stream, gain, counts, fw_one, fw_three, fw_two, mlp_up, mlp_down
):
    head_width = keys.shape[1]
    local_hidden = fw_one.shape[2]
    gate_cols = 2 * local_hidden
    packed_old = jnp.concatenate([fw_one[0], fw_three[0], fw_two[0].T], axis=1)
    first_pre = jnp.dot(keys, fw_one[0].astype(jnp.bfloat16), preferred_element_type=jnp.float32)
    third_pre = jnp.dot(keys, fw_three[0].astype(jnp.bfloat16), preferred_element_type=jnp.float32)
    act_first, slope_first = swish_parts(first_pre)
    hidden_in = (act_first * third_pre).astype(jnp.bfloat16)
    scaled_val = (rates * values.astype(jnp.float32)).astype(jnp.bfloat16)
    second_t = fw_two[0].T.astype(jnp.bfloat16)
    back_hidden = jnp.dot(scaled_val, second_t, preferred_element_type=jnp.float32)
    err_first = (back_hidden * third_pre * slope_first).astype(jnp.bfloat16)
    err_third = (back_hidden * act_first).astype(jnp.bfloat16)
    grad_first = jnp.einsum("nd,nf->df", keys, err_first, preferred_element_type=jnp.float32)
    grad_third = jnp.einsum("nd,nf->df", keys, err_third, preferred_element_type=jnp.float32)
    grad_second = jnp.einsum("nd,nf->df", scaled_val, hidden_in, preferred_element_type=jnp.float32)
    grad_all = lax.psum(
        jnp.concatenate([grad_first, grad_third, grad_second], axis=1).astype(jnp.bfloat16), "tok"
    ).astype(jnp.float32)
    packed_new = packed_old + grad_all
    col_former, col_updated = column_squares(packed_old, packed_new, gate_cols)
    fast = rescale(packed_old, packed_new, col_former, col_updated)
    query_first = jnp.dot(queries, fast[:, :local_hidden], preferred_element_type=jnp.float32)
    query_third = jnp.dot(
        queries, fast[:, local_hidden:gate_cols], preferred_element_type=jnp.float32
    )
    query_act, unused_slope = swish_parts(query_first)
    query_hidden = (query_act * query_third).astype(jnp.bfloat16)
    head_part = jnp.einsum(
        "tf,df->td", query_hidden, fast[:, gate_cols:], preferred_element_type=jnp.float32
    )
    head_out = lax.psum(head_part.astype(jnp.bfloat16), "rep").astype(jnp.float32)
    mixed_rows = stream.astype(jnp.float32) + head_out
    row_total = lax.psum(jnp.sum(mixed_rows * mixed_rows, axis=1), "head")
    model_width = head_width * lax.axis_size("head")
    inv_rms = lax.rsqrt(row_total / model_width + 1e-06)
    normed = (mixed_rows * inv_rms[:, None] * gain).astype(jnp.bfloat16)
    features = lax.all_gather(normed, "head", axis=1, tiled=True)
    up_total = jnp.dot(
        features,
        lax.all_gather(mlp_up, "tok", axis=0, tiled=True),
        preferred_element_type=jnp.float32,
    )
    expanded = jax.nn.gelu(up_total, approximate=False).astype(jnp.bfloat16)
    partial_terms = jnp.dot(
        expanded,
        lax.all_gather(mlp_down, "tok", axis=1, tiled=True),
        preferred_element_type=jnp.float32,
    )
    summed = lax.psum_scatter(
        partial_terms.astype(jnp.bfloat16), ("head", "rep"), scatter_dimension=1, tiled=True
    ).astype(jnp.float32)
    out_width = summed.shape[1]
    stream_cols = lax.dynamic_slice_in_dim(
        mixed_rows, lax.axis_index("rep") * out_width, out_width, 1
    )
    slot_index = jnp.arange(mixed_rows.shape[0], dtype=jnp.int32)
    live_rows = slot_index < counts[0]
    return jnp.where(live_rows[:, None], stream_cols + summed, 0.0).astype(jnp.bfloat16)


def solution(mesh):
    placed = (
        P(("groups", "tok"), "head"),
        P(("groups", "tok"), "head"),
        P(("groups", "tok"), "head"),
        P(("groups", "tok"), "head"),
        P(("groups", "tok"), "head"),
        P("head"),
        P(("groups", "tok")),
        P("head", None, "rep"),
        P("head", None, "rep"),
        P("head", "rep", None),
        P("tok", ("head", "rep")),
        P(("head", "rep"), "tok"),
    )
    return jax.shard_map(
        on_device,
        mesh=mesh,
        in_specs=placed,
        out_specs=P(("groups", "tok"), ("head", "rep")),
        check_vma=False,
    )
```

profile of v0, /device:TPU:0, one launch (start us, length us, event | category | flops | bytes accessed | tf_op | source)
XLA Modules:
  0.0 239.5 jit_solution(2878484344632137081)
XLA Ops:
  6.5 0.0 copy-start
  6.5 0.0 all-reduce.4.cloned.1.call-start
  6.5 1.6 copy.13
  8.1 0.0 copy-start.1
  8.1 0.0 copy-start.3
  8.2 0.0 copy-start.7
  8.2 0.0 copy-start.9
  8.2 2.0 copy.14
  10.1 0.0 copy-done
  10.2 0.0 copy-start.2
  10.2 0.3 fusion.111
  10.5 0.3 fusion.109
  10.8 0.3 fusion.22
  11.1 0.4 convolution_convert_fusion
  11.5 0.4 fusion.1
  11.9 0.3 fusion.2
  12.2 1.2 pad_maximum_fusion
  13.5 0.0 all-reduce.4.cloned.1.call-update
  13.5 0.0 all-reduce.6.cloned.1.call-start
  13.6 0.2 fusion
  13.8 0.1 multiply_reduce_fusion.2
  13.9 71.5 %all-reduce.4.cloned.1.call-done = bf16[512,1536]{0,1:T(8,128)(2,1)} async-done(((bf16[512,1536]{0,1:T(8,128)(2,1)}), bf16[512,1536]{0,1:T(8,128)(2,1)}) %all-reduce.4.cloned.1.call-update) | async-done | bytes 1572880 | tf_op jit(solution)/shard_map/psum | solution.py:50
  85.5 2.9 %maximum_add_fusion = f32[512,1536]{0,1:T(8,128)S(1)} fusion(f32[512,512]{0,1:T(8,128)} %bitcast.75, f32[512,512]{0,1:T(8,128)} %bitcast.74, f32[512,512]{0,1:T(8,128)} %bitcast.72, bf16[512,1536]{0,1:T(8,128)(2,1)} %all-reduce.4.cloned.1.call-done), kind=kLoop, calls=%fused_computation | loop fusion | flops 3145728 | bytes 7864320 | tf_op jit(solution)/shard_map/add | solution.py:53
  88.3 0.2 multiply_reduce_fusion
  88.5 0.0 copy-start.6
  88.5 0.1 multiply_reduce_fusion.1
  88.7 0.3 multiply_convert_fusion
  89.0 1.0 copy-done.4
  90.0 1.0 convolution_bitcast_fusion.1
  91.0 2.6 %all-reduce = (f32[512]{0:T(512)S(1)}, f32[512]{0:T(512)S(1)}) all-reduce(f32[512]{0:T(512)S(1)} %multiply_reduce_fusion.1, f32[512]{0:T(512)S(1)} %multiply_reduce_fusion.2), channel_id=1, replica_groups=mesh['groups'=2,'tok'=4,'head'=2,'rep'=2] {'rep'}, use_global_device_ids=true, to_apply=%region_6.0 | all-reduce | flops 1024 | bytes 8192 | tf_op jit(solution)/shard_map/psum | solution.py:22
  93.6 2.2 convolution_convert_fusion.4
  95.9 0.0 all-reduce.6.cloned.1.call-update
  95.9 0.0 all-gather.3.cloned.1.call-start
  96.0 0.7 all-gather.3.cloned.1.call-update
  96.6 0.0 all-gather.5.cloned.1.call-start
  96.7 0.5 all-gather.5.cloned.1.call-update
  97.2 0.0 reduce-scatter.2.cloned.1.call-start
  97.3 15.8 %all-reduce.6.cloned.1.call-done = bf16[128,512]{1,0:T(8,128)(2,1)} async-done(((bf16[128,512]{1,0:T(8,128)(2,1)}), bf16[128,512]{1,0:T(8,128)(2,1)}) %all-reduce.6.cloned.1.call-update) | async-done | bytes 131088 | tf_op jit(solution)/shard_map/psum | solution.py:65
  113.0 1.0 convert_add_fusion
  114.1 4.9 %psum.39 = f32[128]{0:T(128)S(1)} all-reduce(f32[128]{0:T(128)S(1)} %get-tuple-element.8), channel_id=1, replica_groups=mesh['groups'=2,'tok'=4,'head'=2,'rep'=2] {'head'}, use_global_device_ids=true, to_apply=%region_9.0 | all-reduce | flops 128 | bytes 1024 | tf_op jit(solution)/shard_map/psum | solution.py:67
  119.0 1.0 multiply_convert_fusion.3
  120.0 5.6 %all_gather.9 = bf16[128,1024]{1,0:T(8,128)(2,1)S(1)} all-gather(bf16[128,512]{1,0:T(8,128)(2,1)S(1)} %multiply_convert_fusion.3), channel_id=1, replica_groups=mesh['groups'=2,'tok'=4,'head'=2,'rep'=2] {'head'}, dimensions={1}, use_global_device_ids=true | all-gather | bytes 393216 | tf_op jit(solution)/shard_map/all_gather | solution.py:71
  125.7 36.1 %all-gather.3.cloned.1.call-done = bf16[1024,1024]{1,0:T(8,128)(2,1)} async-done(((bf16[256,1024]{1,0:T(8,128)(2,1)}), bf16[1024,1024]{1,0:T(8,128)(2,1)}) %all-gather.3.cloned.1.call-update) | async-done | bytes 2097168 | tf_op jit(solution)/shard_map/all_gather | solution.py:74
  161.7 46.4 %all-gather.5.cloned.1.call-done = bf16[1024,1024]{1,0:T(8,128)(2,1)} async-done(((bf16[1024,256]{1,0:T(8,128)(2,1)}), bf16[1024,1024]{1,0:T(8,128)(2,1)}) %all-gather.5.cloned.1.call-update) | async-done | bytes 2097168 | tf_op jit(solution)/shard_map/all_gather | solution.py:80
  208.1 4.8 %convolution_convert_fusion.3 = bf16[128,1024]{1,0:T(8,128)(2,1)} fusion(bf16[1024,1024]{1,0:T(8,128)(2,1)} %all-gather.5.cloned.1.call-done, bf16[128,1024]{1,0:T(8,128)(2,1)S(1)} %all_gather.9, bf16[1024,1024]{1,0:T(8,128)(2,1)} %all-gather.3.cloned.1.call-done), kind=kOutput, calls=%fused_computation.11 | convolution fusion | flops 545521664 | bytes 4718592 | tf_op jit(solution)/shard_map/dot_general | solution.py:78
  212.9 0.0 reduce-scatter.2.cloned.1.call-update
  213.6 17.8 %reduce-scatter.2.cloned.1.call-done = bf16[128,256]{1,0:T(8,128)(2,1)} async-done(((bf16[128,1024]{1,0:T(8,128)(2,1)}), bf16[128,256]{1,0:T(8,128)(2,1)}) %reduce-scatter.2.cloned.1.call-update) | async-done | bytes 65552 | tf_op jit(solution)/shard_map/reduce_scatter | solution.py:83
  231.4 1.6 select_convert_fusion
  (16 shorter events, 0.1 us)
Async XLA Ops:
  6.5 3.6 %copy-start = (bf16[128,512]{1,0:T(8,128)(2,1)S(1)}, bf16[128,512]{1,0:T(8,128)(2,1)}, u32[]{:S(2)}) copy-start(bf16[128,512]{1,0:T(8,128)(2,1)} %param.12) | copy-start | bytes 393220
  6.5 78.9 %all-reduce.4.cloned.1.call-start = ((), (), s32[]{:S(2)}) async-start(), calls=%async_computation.1 | async-start | bytes 3145728 | tf_op jit(solution)/shard_map/psum | solution.py:50
  8.1 5.4 %copy-start.1 = (f32[1,512,512]{1,2,0:T(8,128)}, f32[1,512,512]{1,2,0:T(8,128)S(1)}, u32[]{:S(2)}) copy-start(f32[1,512,512]{1,2,0:T(8,128)S(1)} %copy.13) | copy-start | bytes 3145732
  8.1 2.6 %copy-start.3 = (f32[1,512,512]{2,1,0:T(8,128)S(1)}, f32[1,512,512]{2,1,0:T(8,128)}, u32[]{:S(2)}) copy-start(f32[1,512,512]{2,1,0:T(8,128)} %param.21) | copy-start | bytes 3145732
  8.2 2.6 %copy-start.7 = (bf16[128,512]{1,0:T(8,128)(2,1)S(1)}, bf16[128,512]{1,0:T(8,128)(2,1)}, u32[]{:S(2)}) copy-start(bf16[128,512]{1,0:T(8,128)(2,1)} %param.13) | copy-start | bytes 393220
  8.2 2.6 %copy-start.9 = (f32[128,1]{0,1:T(1,128)S(1)}, f32[128,1]{0,1:T(1,128)}, u32[]{:S(2)}) copy-start(f32[128,1]{0,1:T(1,128)} %param.14) | copy-start | bytes 1540
  10.2 3.4 %copy-start.2 = (f32[1,512,512]{1,2,0:T(8,128)}, f32[1,512,512]{1,2,0:T(8,128)S(1)}, u32[]{:S(2)}) copy-start(f32[1,512,512]{1,2,0:T(8,128)S(1)} %copy.14) | copy-start | bytes 3145732
  13.5 99.5 %all-reduce.6.cloned.1.call-start = ((), (), s32[]{:S(2)}) async-start(), calls=%async_computation.2 | async-start | bytes 262144 | tf_op jit(solution)/shard_map/psum | solution.py:65
  88.5 1.5 copy-start.6
  89.0 1.0 copy-start.4
  91.0 22.0 %copy-start.5 = (bf16[128,512]{1,0:T(8,128)(2,1)S(1)}, bf16[128,512]{1,0:T(8,128)(2,1)}, u32[]{:S(2)}) copy-start(bf16[128,512]{1,0:T(8,128)(2,1)} %param.16) | copy-start | bytes 393220
  93.6 25.4 %copy-start.8 = (f32[512]{0:T(512)S(1)}, f32[512]{0:T(512)}, u32[]{:S(2)}) copy-start(f32[512]{0:T(512)} %param.17) | copy-start | bytes 6148
  95.9 65.8 %all-gather.3.cloned.1.call-start = ((), (), s32[]{:S(2)}) async-start(), calls=%async_computation.3 | async-start | bytes 2621440 | tf_op jit(solution)/shard_map/all_gather | solution.py:74
  96.6 111.5 %all-gather.5.cloned.1.call-start = ((), (), s32[]{:S(2)}) async-start(), calls=%async_computation.4 | async-start | bytes 2621440 | tf_op jit(solution)/shard_map/all_gather | solution.py:80
  97.2 134.2 %reduce-scatter.2.cloned.1.call-start = ((), (), s32[]{:S(2)}) async-start(), calls=%async_computation.5 | async-start | bytes 327680 | tf_op jit(solution)/shard_map/reduce_scatter | solution.py:83
Sparse Core Ops, SparseCore 0:
  13.6 71.7 all-reduce.3
  96.0 16.9 all-reduce.5
  114.6 47.0 all-gather.2
  163.2 44.9 all-gather.4
  213.1 18.2 reduce-scatter.1
where the time goes:
time: 240 us; the launch traced here: 239 us
  waiting for transfers between devices  189 us (79%)
  between operations  14 us (6%)
  blocking collectives  13.2 us (6%)
  matrix products  10 us (4%)
  other arithmetic  8.71 us (4%)
  local copies, waits for them, and re-layouts  4.58 us (2%)
    psum x1, waiting for transfers between devices, on_device(): lax.psum(jnp.concatenate([grad_first, grad_third, grad_second], axis=1).a...  71.5 us
    all_gather x1, waiting for transfers between devices, on_device(): lax.all_gather(mlp_down, 'tok', axis=1, tiled=True)  46.4 us
    all_gather x1, waiting for transfers between devices, on_device(): lax.all_gather(mlp_up, 'tok', axis=0, tiled=True)  36.1 us
    reduce_scatter x1, waiting for transfers between devices, on_device(): lax.psum_scatter(partial_terms.astype(jnp.bfloat16), ('head', 'rep'), sca...  17.8 us
    psum x1, waiting for transfers between devices, on_device(): lax.psum(head_part.astype(jnp.bfloat16), 'rep').astype(jnp.float32)  15.8 us
    all_gather x1, blocking collectives, on_device(): features = lax.all_gather(normed, 'head', axis=1, tiled=True)  5.64 us
    psum x1, blocking collectives, on_device(): row_total = lax.psum(jnp.sum(mixed_rows * mixed_rows, axis=1), 'head')  4.93 us
  transfers between devices with their start and end apart: 5, of which 5 were waited for; matrix products, arithmetic and copies ran while one was open for 1% of the time, Pallas kernels for 0%

commit v1 on v0

--- a/solution.py
+++ b/solution.py
@@ -62,7 +62,9 @@
     head_part = jnp.einsum(
         "tf,df->td", query_hidden, fast[:, gate_cols:], preferred_element_type=jnp.float32
     )
-    head_out = lax.psum(head_part.astype(jnp.bfloat16), "rep").astype(jnp.float32)
+    head_out = jnp.sum(lax.all_gather(head_part.astype(jnp.bfloat16), "rep"), axis=0).astype(
+        jnp.float32
+    )
     mixed_rows = stream.astype(jnp.float32) + head_out
     row_total = lax.psum(jnp.sum(mixed_rows * mixed_rows, axis=1), "head")
     model_width = head_width * lax.axis_size("head")

time: 240 us -> 210 us (0.88)
  waiting for transfers between devices: 189 us -> 159 us
    psum x1 -> x0, waiting for transfers between devices: 15.8 us -> none  [on_device(): lax.psum(head_part.astype(jnp.bfloat16), 'rep').astype(jnp.float32)]
    all_gather x1, waiting for transfers between devices: 36.1 us -> 23.2 us  [on_device(): lax.all_gather(mlp_up, 'tok', axis=0, tiled=True)]
  transfers between devices with their start and end apart: 5 -> 4, of which waited for: 5 -> 4; matrix products, arithmetic and copies ran while one was open for 1% -> 4% of each run, Pallas kernels for 0% -> 0%
where the time goes in v1:
time: 210 us
  waiting for transfers between devices  159 us (76%)
  blocking collectives  15.2 us (7%)
  between operations  14 us (7%)
  matrix products  10.1 us (5%)
  other arithmetic  6.99 us (3%)
  local copies, waits for them, and re-layouts  4.56 us (2%)
    psum x1, waiting for transfers between devices, on_device(): lax.psum(jnp.concatenate([grad_first, grad_third, grad_second], axis=1).a...  70.1 us
    all_gather x1, waiting for transfers between devices, on_device(): lax.all_gather(mlp_down, 'tok', axis=1, tiled=True)  46.6 us
    all_gather x1, waiting for transfers between devices, on_device(): lax.all_gather(mlp_up, 'tok', axis=0, tiled=True)  23.2 us
    reduce_scatter x1, waiting for transfers between devices, on_device(): lax.psum_scatter(partial_terms.astype(jnp.bfloat16), ('head', 'rep'), sca...  17.8 us
    all_gather x1, blocking collectives, on_device(): features = lax.all_gather(normed, 'head', axis=1, tiled=True)  5.64 us
    psum x1, blocking collectives, on_device(): row_total = lax.psum(jnp.sum(mixed_rows * mixed_rows, axis=1), 'head')  4.93 us
    dot_general x1, matrix products, on_device(): jnp.dot(expanded, lax.all_gather(mlp_down, 'tok', axis=1, tiled=True), pr...  4.77 us
    unnamed x22, local copies, waits for them, and re-layouts  4.56 us
  transfers between devices with their start and end apart: 4, of which 4 were waited for; matrix products, arithmetic and copies ran while one was open for 4% of the time, Pallas kernels for 0%

profile of v1, /device:TPU:0, one launch (start us, length us, event | category | flops | bytes accessed | tf_op | source)
XLA Modules:
  0.0 210.0 jit_solution(7992206436708411710)
XLA Ops:
  6.5 0.0 copy-start
  6.5 0.0 all-reduce.3.cloned.1.call-start
  6.5 1.6 copy.13
  8.1 0.0 copy-start.1
  8.1 0.0 copy-start.3
  8.2 0.0 copy-start.7
  8.2 0.0 copy-start.9
  8.2 2.0 copy.14
  10.1 0.0 copy-done
  10.2 0.0 copy-start.2
  10.2 0.3 fusion.111
  10.5 0.3 fusion.109
  10.8 0.0 copy-done.3
  10.8 0.3 fusion.22
  11.1 0.4 convolution_convert_fusion
  11.5 0.4 fusion.1
  11.9 0.3 fusion.2
  12.2 1.3 pad_maximum_fusion
  13.5 0.0 all-reduce.3.cloned.1.call-update
  13.5 0.0 all-gather.4.cloned.1.call-start
  13.6 0.7 all-gather.4.cloned.1.call-update
  14.3 0.0 all-gather.6.cloned.1.call-start
  14.3 0.7 all-gather.6.cloned.1.call-update
  15.0 0.0 reduce-scatter.2.cloned.1.call-start
  15.1 0.1 multiply_reduce_fusion.2
  15.2 0.2 fusion
  15.4 70.1 %all-reduce.3.cloned.1.call-done = bf16[512,1536]{0,1:T(8,128)(2,1)} async-done(((bf16[512,1536]{0,1:T(8,128)(2,1)}), bf16[512,1536]{0,1:T(8,128)(2,1)}) %all-reduce.3.cloned.1.call-update) | async-done | bytes 1572880 | tf_op jit(solution)/shard_map/psum | solution.py:50
  85.5 2.9 %maximum_add_fusion = f32[512,1536]{0,1:T(8,128)S(1)} fusion(f32[512,512]{0,1:T(8,128)} %bitcast.76, f32[512,512]{0,1:T(8,128)} %bitcast.75, f32[512,512]{0,1:T(8,128)} %bitcast.73, bf16[512,1536]{0,1:T(8,128)(2,1)} %all-reduce.3.cloned.1.call-done), kind=kLoop, calls=%fused_computation | loop fusion | flops 3145728 | bytes 7864320 | tf_op jit(solution)/shard_map/add | solution.py:53
  88.4 0.1 multiply_reduce_fusion.1
  88.5 2.5 %all-reduce = (f32[512]{0:T(512)S(1)}, f32[512]{0:T(512)S(1)}) all-reduce(f32[512]{0:T(512)S(1)} %multiply_reduce_fusion.1, f32[512]{0:T(512)S(1)} %multiply_reduce_fusion.2), channel_id=1, replica_groups=mesh['groups'=2,'tok'=4,'head'=2,'rep'=2] {'rep'}, use_global_device_ids=true, to_apply=%region_6.0 | all-reduce | flops 1024 | bytes 8192 | tf_op jit(solution)/shard_map/psum | solution.py:22
  90.9 0.2 multiply_reduce_fusion
  91.2 0.0 copy-start.6
  91.2 0.3 multiply_convert_fusion
  91.6 1.0 copy-done.4
  92.5 1.0 convolution_bitcast_fusion.1
  93.5 2.3 %convolution_convert_fusion.4 = bf16[128,512]{1,0:T(8,128)(2,1)} fusion(bf16[128,512]{1,0:T(8,128)(2,1)S(1)} %copy-done.6, f32[512,1536]{0,1:T(8,128)S(1)} %maximum_add_fusion, bf16[512,1024]{0,1:T(8,128)(2,1)} %copy-done.4, f32[512]{0:T(512)S(1)} %rsqrt_multiply_fusion, f32[128,512]{1,0:T(8,128)} %convolution_bitcast_fusion.1), kind=kOutput, calls=%fused_computation.16 | convolution fusion | flops 135200768 | bytes 2099200 | tf_op jit(solution)/shard_map/tf,df->td/dot_general | solution.py:62
  95.8 2.2 %all-gather = bf16[256,512]{1,0:T(8,128)(2,1)S(1)} all-gather(bf16[128,512]{1,0:T(8,128)(2,1)} %convolution_convert_fusion.4), channel_id=2, replica_groups=mesh['groups'=2,'tok'=4,'head'=2,'rep'=2] {'rep'}, dimensions={0}, use_global_device_ids=true | all-gather | bytes 393216 | tf_op jit(solution)/shard_map/all_gather | solution.py:65
  98.1 0.0 copy-done.5
  98.1 0.1 convert_add_fusion
  98.2 4.9 %psum.31 = f32[128]{0:T(128)S(1)} all-reduce(f32[128]{0:T(128)S(1)} %get-tuple-element.8), channel_id=1, replica_groups=mesh['groups'=2,'tok'=4,'head'=2,'rep'=2] {'head'}, use_global_device_ids=true, to_apply=%region_9.0 | all-reduce | flops 128 | bytes 1024 | tf_op jit(solution)/shard_map/psum | solution.py:69
  103.2 0.1 multiply_convert_fusion.3
  103.3 5.6 %all_gather.17 = bf16[128,1024]{1,0:T(8,128)(2,1)S(1)} all-gather(bf16[128,512]{1,0:T(8,128)(2,1)S(1)} %multiply_convert_fusion.3), channel_id=1, replica_groups=mesh['groups'=2,'tok'=4,'head'=2,'rep'=2] {'head'}, dimensions={1}, use_global_device_ids=true | all-gather | bytes 393216 | tf_op jit(solution)/shard_map/all_gather | solution.py:73
  108.9 23.2 %all-gather.4.cloned.1.call-done = bf16[1024,1024]{1,0:T(8,128)(2,1)} async-done(((bf16[256,1024]{1,0:T(8,128)(2,1)}), bf16[1024,1024]{1,0:T(8,128)(2,1)}) %all-gather.4.cloned.1.call-update) | async-done | bytes 2097168 | tf_op jit(solution)/shard_map/all_gather | solution.py:76
  132.1 46.6 %all-gather.6.cloned.1.call-done = bf16[1024,1024]{1,0:T(8,128)(2,1)} async-done(((bf16[1024,256]{1,0:T(8,128)(2,1)}), bf16[1024,1024]{1,0:T(8,128)(2,1)}) %all-gather.6.cloned.1.call-update) | async-done | bytes 2097168 | tf_op jit(solution)/shard_map/all_gather | solution.py:82
  178.7 4.8 %convolution_convert_fusion.3 = bf16[128,1024]{1,0:T(8,128)(2,1)} fusion(bf16[1024,1024]{1,0:T(8,128)(2,1)} %all-gather.6.cloned.1.call-done, bf16[128,1024]{1,0:T(8,128)(2,1)S(1)} %all_gather.17, bf16[1024,1024]{1,0:T(8,128)(2,1)} %all-gather.4.cloned.1.call-done), kind=kOutput, calls=%fused_computation.11 | convolution fusion | flops 545521664 | bytes 4718592 | tf_op jit(solution)/shard_map/dot_general | solution.py:80
  183.4 0.0 reduce-scatter.2.cloned.1.call-update
  184.1 17.8 %reduce-scatter.2.cloned.1.call-done = bf16[128,256]{1,0:T(8,128)(2,1)} async-done(((bf16[128,1024]{1,0:T(8,128)(2,1)}), bf16[128,256]{1,0:T(8,128)(2,1)}) %reduce-scatter.2.cloned.1.call-update) | async-done | bytes 65552 | tf_op jit(solution)/shard_map/reduce_scatter | solution.py:85
  201.9 1.6 select_convert_fusion
  (15 shorter events, 0.1 us)
Async XLA Ops:
  6.5 3.6 %copy-start = (bf16[128,512]{1,0:T(8,128)(2,1)S(1)}, bf16[128,512]{1,0:T(8,128)(2,1)}, u32[]{:S(2)}) copy-start(bf16[128,512]{1,0:T(8,128)(2,1)} %param.12) | copy-start | bytes 393220
  6.5 79.0 %all-reduce.3.cloned.1.call-start = ((), (), s32[]{:S(2)}) async-start(), calls=%async_computation.1 | async-start | bytes 3145728 | tf_op jit(solution)/shard_map/psum | solution.py:50
  8.1 7.1 %copy-start.1 = (f32[1,512,512]{1,2,0:T(8,128)}, f32[1,512,512]{1,2,0:T(8,128)S(1)}, u32[]{:S(2)}) copy-start(f32[1,512,512]{1,2,0:T(8,128)S(1)} %copy.13) | copy-start | bytes 3145732
  8.1 2.6 %copy-start.3 = (f32[1,512,512]{2,1,0:T(8,128)S(1)}, f32[1,512,512]{2,1,0:T(8,128)}, u32[]{:S(2)}) copy-start(f32[1,512,512]{2,1,0:T(8,128)} %param.21) | copy-start | bytes 3145732
  8.2 2.6 %copy-start.7 = (bf16[128,512]{1,0:T(8,128)(2,1)S(1)}, bf16[128,512]{1,0:T(8,128)(2,1)}, u32[]{:S(2)}) copy-start(bf16[128,512]{1,0:T(8,128)(2,1)} %param.13) | copy-start | bytes 393220
  8.2 2.6 %copy-start.9 = (f32[128,1]{0,1:T(1,128)S(1)}, f32[128,1]{0,1:T(1,128)}, u32[]{:S(2)}) copy-start(f32[128,1]{0,1:T(1,128)} %param.14) | copy-start | bytes 1540
  10.2 5.0 %copy-start.2 = (f32[1,512,512]{1,2,0:T(8,128)}, f32[1,512,512]{1,2,0:T(8,128)S(1)}, u32[]{:S(2)}) copy-start(f32[1,512,512]{1,2,0:T(8,128)S(1)} %copy.14) | copy-start | bytes 3145732
  13.5 118.6 %all-gather.4.cloned.1.call-start = ((), (), s32[]{:S(2)}) async-start(), calls=%async_computation.2 | async-start | bytes 2621440 | tf_op jit(solution)/shard_map/all_gather | solution.py:76
  14.3 164.4 %all-gather.6.cloned.1.call-start = ((), (), s32[]{:S(2)}) async-start(), calls=%async_computation.3 | async-start | bytes 2621440 | tf_op jit(solution)/shard_map/all_gather | solution.py:82
  15.0 186.9 %reduce-scatter.2.cloned.1.call-start = ((), (), s32[]{:S(2)}) async-start(), calls=%async_computation.4 | async-start | bytes 327680 | tf_op jit(solution)/shard_map/reduce_scatter | solution.py:85
  91.2 1.4 copy-start.6
  91.5 1.0 copy-start.4
  92.5 5.5 %copy-start.5 = (bf16[128,512]{1,0:T(8,128)(2,1)S(1)}, bf16[128,512]{1,0:T(8,128)(2,1)}, u32[]{:S(2)}) copy-start(bf16[128,512]{1,0:T(8,128)(2,1)} %param.16) | copy-start | bytes 393220
  93.5 9.6 %copy-start.8 = (f32[512]{0:T(512)S(1)}, f32[512]{0:T(512)}, u32[]{:S(2)}) copy-start(f32[512]{0:T(512)} %param.17) | copy-start | bytes 6148
Sparse Core Ops, SparseCore 0:
  13.7 71.7 all-reduce.2
  87.1 44.9 all-gather.3
  133.7 44.9 all-gather.5
  183.6 18.2 reduce-scatter.1
